TPU v7x, 256 devices: a whole 4x4x8 slice. The times are simulated.
256 devices in a mesh: facet: 16 (over z, core), row: 8 (over x_hi, y), sub: 2 (over x_lo).
Axes of the slice: x: 4 (x_hi: 2, x_lo: 2; x = x_hi * 2 + x_lo), y: 4, z: 8, core: 2. Of those that a mesh axis runs over, the one named last changes fastest.
Arguments:
- facet_model: bfloat16 [2, 4, 8192, 8192], P(None, 'sub', ('facet', 'row')), may hold values from -6 to 6
- sub_offsets: int32 [256], replicated, may hold values from 0 to 65535
- tile_rows: int32 [256, 4], P(('facet', 'row', 'sub')), may hold values from 0 to 120
- tile_counts: int32 [256], P(('facet', 'row', 'sub')), may hold values from 1 to 4, as said below
- visibilities: bfloat16 [256, 4, 32, 8, 256], P(('facet', 'row', 'sub')), may hold values from -6 to 6
Outputs:
- residual_facets: bfloat16 [2, 4, 8192, 8192], P(None, 'sub', ('facet', 'row'))
- residual_vis: bfloat16 [256, 4, 32, 8, 256], P(('facet', 'row', 'sub'))
Inputs may be any that keep to these rules, and one draw needn't show every extreme that they name: tile_counts[s] tiles of subgrid s are live, the first ones; some subgrid has all 4 tiles live. Tile j of subgrid s covers subgrid rows tile_rows[s, j] to tile_rows[s, j] + 7; tiles may intersect.
All inputs are finite; a program needn't handle non-finite values.
Results may differ from a plain program's by a relative error of at most 0.014.
Values may be sent and summed in bfloat16 or wider, within the bound.
No kernel may reach another device: no remote copies, remote signals or barrier semaphores. Data moves between devices by JAX's collectives and lax.ppermute only.
A program may use at most 128 MiB of HBM per device.

v0:
```python
import math
import jax
import jax.numpy as jnp
from jax import lax
from jax.sharding import PartitionSpec as P

SKY = 65536
CS = 64
SG = 128
two_pi = 2.0 * math.pi


def modmul(left, right, modulus):
    lower = right % 256
    upper = right // 256
    return (left * lower % modulus + left * upper % modulus * 256) % modulus


def window_taper(pixels):
    places = jnp.arange(pixels, dtype=jnp.float32)
    curve = jnp.sin(math.pi * (places + 0.5) / pixels)
    return 0.25 + 0.75 * curve * curve


def turn_pair(phase_index, modulus):
    angle = phase_index.astype(jnp.float32) * (-two_pi / modulus)
    return (jnp.cos(angle), jnp.sin(angle))


def column_table(facet_ids, pixels, width, modulus, ratio):
    spacing = modulus // pixels
    column_pos = facet_ids // ratio % ratio * pixels
    freqs = spacing * jnp.arange(width, dtype=jnp.int32)
    places = (column_pos[:, None] + jnp.arange(pixels, dtype=jnp.int32)[None, :]) % modulus
    cosine, sine = turn_pair(modmul(freqs[None, :, None], places[:, None, :], modulus), modulus)
    scaled = window_taper(pixels) / math.sqrt(pixels)
    return (jnp.stack([cosine, sine], axis=1) * scaled).astype(jnp.bfloat16)


def row_block(offsets, pixels, width, modulus, count):
    spacing = modulus // pixels
    freqs = (offsets[:, None] + spacing * jnp.arange(width, dtype=jnp.int32)[None, :]) % modulus
    places = jnp.arange(count, dtype=jnp.int32)
    cosine, sine = turn_pair(modmul(freqs[:, :, None], places[None, None, :], modulus), modulus)
    curve = jnp.sin(math.pi * (places.astype(jnp.float32) + 0.5) / pixels)
    scaled = (0.25 + 0.75 * curve * curve) / math.sqrt(pixels)
    return ((jnp.stack([cosine, sine], axis=1) * scaled).astype(jnp.bfloat16), freqs)


def facet_turn(freqs, facet_ids, modulus, pixels, ratio):
    row_pos = facet_ids % ratio * pixels
    return turn_pair(modmul(freqs[:, :, None], row_pos[None, None, :], modulus), modulus)


def grid_table(size):
    places = jnp.arange(size, dtype=jnp.int32)
    angle = (places[:, None] * places[None, :] % size).astype(jnp.float32) * (two_pi / size)
    return (jnp.stack([jnp.cos(angle), jnp.sin(angle)]) / math.sqrt(size)).astype(jnp.bfloat16)


def slot_table(count, ratio):
    facet_ids = jnp.arange(count, dtype=jnp.int32)
    first = facet_ids % ratio
    second = facet_ids // ratio % ratio
    options = jnp.arange(ratio, dtype=jnp.int32)
    hits = (first[:, None, None] == options[None, :, None]) & (
        second[:, None, None] == options[None, None, :]
    )
    return hits.astype(jnp.bfloat16)


def finish_contrib(raw, turn_real, turn_imag):
    part_real = raw[:, 0, :, :, :, 0] - raw[:, 1, :, :, :, 1]
    part_imag = raw[:, 0, :, :, :, 1] + raw[:, 1, :, :, :, 0]
    real_turn = turn_real[:, :, :, None, None]
    imag_turn = turn_imag[:, :, :, None, None]
    out_real = real_turn * part_real - imag_turn * part_imag
    out_imag = real_turn * part_imag + imag_turn * part_real
    joined = jnp.stack([out_real, out_imag], axis=4)
    return jnp.transpose(joined, (0, 2, 3, 1, 4, 5)).astype(jnp.bfloat16)


def assemble(contrib, slots, grid):
    width = contrib.shape[2]
    terms = contrib.shape[1]
    ratio = slots.shape[1]
    size = width * ratio
    placed = jnp.einsum("fab,ftkcl->katclb", slots, contrib, preferred_element_type=jnp.float32)
    amatrix = placed.reshape(size, terms, 2, size).astype(jnp.bfloat16)
    first = jnp.einsum("zum,mtcn->zutcn", grid, amatrix, preferred_element_type=jnp.float32)
    front = jnp.stack(
        [first[0, :, :, 0] - first[1, :, :, 1], first[0, :, :, 1] + first[1, :, :, 0]], axis=2
    ).astype(jnp.bfloat16)
    second = jnp.einsum("utcn,zvn->utczv", front, grid, preferred_element_type=jnp.float32)
    sky_real = second[:, :, 0, 0] - second[:, :, 1, 1]
    sky_imag = second[:, :, 0, 1] + second[:, :, 1, 0]
    return jnp.stack([sky_real, sky_imag], axis=2).astype(jnp.bfloat16)


def degrid_grid(sky_grid, rows, count, observed):
    slots_count, channels, tile_height, span = observed.shape
    size = sky_grid.shape[0]
    nu_values = (jnp.arange(channels, dtype=jnp.float32) + 0.5) / channels - 0.5
    live = jnp.arange(slots_count, dtype=jnp.int32) < count
    target = rows[:, None] + jnp.arange(tile_height, dtype=jnp.int32)[None, :]
    hits = (target[:, :, None] == jnp.arange(size, dtype=jnp.int32)[None, None, :]) & live[
        :, None, None
    ]
    placer = hits.astype(jnp.bfloat16).reshape(slots_count * tile_height, size)
    model_rows = jnp.dot(
        placer, sky_grid.reshape(size, 2 * span), preferred_element_type=jnp.float32
    )
    model_rows = model_rows.reshape(slots_count, tile_height, 2, span)
    model = model_rows[:, None, :, 0] + nu_values[None, :, None, None] * model_rows[:, None, :, 1]
    residual = (observed.astype(jnp.float32) - model) * live[:, None, None, None].astype(
        jnp.float32
    )
    weighted = jnp.stack(
        [jnp.sum(residual, axis=1), jnp.sum(nu_values[None, :, None, None] * residual, axis=1)],
        axis=2,
    )
    weighted = weighted.astype(jnp.bfloat16).reshape(slots_count * tile_height, 2 * span)
    regrid = lax.dot_general(
        placer, weighted, (((0,), (0,)), ((), ())), preferred_element_type=jnp.float32
    )
    return (residual.astype(jnp.bfloat16), regrid.reshape(size, 2, 2, size).astype(jnp.bfloat16))


def adjoint_grid(regrid, grid):
    first = jnp.einsum("zum,utcv->zmtcv", grid, regrid, preferred_element_type=jnp.float32)
    back_real = first[0, :, :, 0] + first[1, :, :, 1]
    back_imag = first[0, :, :, 1] - first[1, :, :, 0]
    back_front = jnp.stack([back_real, back_imag], axis=2).astype(jnp.bfloat16)
    second = jnp.einsum("mtcv,zvn->mtczn", back_front, grid, preferred_element_type=jnp.float32)
    grid_real = second[:, :, 0, 0] + second[:, :, 1, 1]
    grid_imag = second[:, :, 1, 0] - second[:, :, 0, 1]
    return jnp.stack([grid_real, grid_imag], axis=2).astype(jnp.bfloat16)


def select_slots(back_grid, slots):
    ratio = slots.shape[1]
    size = back_grid.shape[0]
    width = size // ratio
    terms = back_grid.shape[1]
    shaped = back_grid.reshape(width, ratio, terms, 2, width, ratio)
    return jnp.einsum(
        "fab,katclb->ftkcl", slots, shaped, preferred_element_type=jnp.float32
    ).astype(jnp.bfloat16)


def turn_back(returned, turn_real, turn_imag):
    real_turn = jnp.transpose(turn_real, (0, 2, 1))[:, :, None, :, None]
    imag_turn = jnp.transpose(turn_imag, (0, 2, 1))[:, :, None, :, None]
    part_real = returned[:, :, :, :, 0].astype(jnp.float32)
    part_imag = returned[:, :, :, :, 1].astype(jnp.float32)
    turned = jnp.stack(
        [
            real_turn * part_real + imag_turn * part_imag,
            real_turn * part_imag - imag_turn * part_real,
        ],
        axis=4,
    )
    return turned.astype(jnp.bfloat16)


def paired_terms(turned):
    real_part = turned[:, :, :, :, 0]
    imag_part = turned[:, :, :, :, 1]
    pair_real = jnp.stack([real_part, imag_part], axis=1)
    pair_imag = jnp.stack([imag_part, -real_part], axis=1)
    return jnp.stack([pair_real, pair_imag], axis=5)


def strip_terms(table_part, paired):
    return jnp.einsum("szkp,szftkcl->pftcl", table_part, paired, preferred_element_type=jnp.float32)


def local(facet_model, sub_offsets, tile_rows, tile_counts, visibilities):
    facets_here = facet_model.shape[1]
    pixels = facet_model.shape[3]
    ratio = SG // CS
    pairs = lax.axis_size("sub")
    pair = lax.axis_index("sub")
    strip_group = lax.axis_index(("facet", "row"))
    facet_total = facets_here * pairs
    local_facets = pair * facets_here + jnp.arange(facets_here, dtype=jnp.int32)
    columns = column_table(local_facets, pixels, CS, SKY, ratio)
    strips = jnp.einsum(
        "tfpq,fckq->pftck", facet_model, columns, preferred_element_type=jnp.float32
    ).astype(jnp.bfloat16)
    group_offsets = lax.dynamic_slice_in_dim(sub_offsets, strip_group * pairs, pairs, 0)
    rtable, freqs = row_block(group_offsets, pixels, CS, SKY, pixels)
    turn_real, turn_imag = facet_turn(freqs, local_facets, SKY, pixels, ratio)
    table_part = rtable
    raw = jnp.einsum(
        "szkp,pftcl->szkftcl",
        table_part,
        lax.all_gather(strips, ("facet", "row"), axis=0, tiled=True),
        preferred_element_type=jnp.float32,
    )
    contrib = finish_contrib(raw, turn_real, turn_imag)
    slots = slot_table(facet_total, ratio)
    grid = grid_table(SG)
    sky_grid = assemble(
        lax.all_to_all(contrib, "sub", split_axis=0, concat_axis=1, tiled=True)[0], slots, grid
    )
    residual, regrid = degrid_grid(sky_grid, tile_rows[0], tile_counts[0], visibilities[0])
    back_grid = adjoint_grid(regrid, grid)
    returned = select_slots(back_grid, slots)[None]
    received = lax.all_to_all(returned, "sub", split_axis=1, concat_axis=0, tiled=True)
    turned = turn_back(received, turn_real, turn_imag)
    paired = paired_terms(turned)
    table_part = rtable
    mine = lax.psum_scatter(
        strip_terms(table_part, paired), ("facet", "row"), scatter_dimension=0, tiled=True
    )
    strip_round = mine.astype(jnp.bfloat16)
    residual_facets = jnp.einsum(
        "pftck,fckq->tfpq", strip_round, columns, preferred_element_type=jnp.float32
    ).astype(jnp.bfloat16)
    return (residual_facets, residual[None])


def solution(mesh):
    placed = (
        P(None, "sub", ("facet", "row"), None),
        P(),
        P(("facet", "row", "sub"), None),
        P(("facet", "row", "sub")),
        P(("facet", "row", "sub"), None, None, None, None),
    )
    return jax.shard_map(
        local,
        mesh=mesh,
        in_specs=placed,
        out_specs=(
            P(None, "sub", ("facet", "row"), None),
            P(("facet", "row", "sub"), None, None, None, None),
        ),
        check_vma=False,
    )
```

profile of v0, /device:TPU:2, one launch (start us, length us, event | category | flops | bytes accessed | tf_op | source)
XLA Modules:
  0.0 1020.6 jit_solution(10398024351297575194)
XLA Ops:
  7.4 0.4 and_select_fusion.1
  7.8 19.9 %fusion.28 = (f32[2,1,64,8192]{3,2,1,0:T(8,128)S(1)}, f32[2,1,64,8192]{3,2,1,0:T(8,128)S(1)}) fusion(s32[2,8192]{1,0:T(2,128)S(1)} %get-tuple-element.37, s32[2,8192]{1,0:T(2,128)S(1)} %get-tuple-element.36, s32[64]{0:T(128)S(1)} %iota_multiply_fusion), kind=kLoop, calls=%fused_computation.58 | loop fusion | flops 40894464 | bytes 8519936 | tf_op jit(solution)/shard_map/cos | solution.py:27
  27.8 2.0 copy-done
  29.7 1.3 copy-done.1
  31.1 2.3 fusion.36
  33.3 0.8 copy.122
  35.4 0.3 fusion.104
  35.9 21.4 %fusion.26 = (f32[2,1,64,8192]{3,2,1,0:T(8,128)}, f32[2,1,64,8192]{3,2,1,0:T(8,128)}) fusion(s32[8192]{0:T(1024)S(1)} %get-tuple-element.44, s32[8192]{0:T(1024)S(1)} %get-tuple-element.45, s32[2,64]{1,0:T(2,128)S(1)} %and_select_fusion.15), kind=kLoop, calls=%fused_computation.56 | loop fusion | flops 40894464 | bytes 8454656 | tf_op jit(solution)/shard_map/cos | solution.py:27
  57.3 130.4 %all-gather.2.cloned.1.call-done = bf16[8192,2,2,2,64]{4,3,2,1,0:T(2,128)(2,1)} async-done(((bf16[64,2,2,2,64]{4,3,2,1,0:T(2,128)(2,1)}), bf16[8192,2,2,2,64]{4,3,2,1,0:T(2,128)(2,1)}) %all-gather.2.cloned.1.call-update) | async-done | bytes 8388624 | tf_op jit(solution)/shard_map/all_gather | solution.py:198
  187.7 10.6 %fusion = f32[2,2,64,2,2,2,64]{6,2,5,4,3,1,0:T(8,128)S(1)} fusion(bf16[8192,2,2,2,64,1,1]{4,3,2,1,0,6,5:T(2,128)(2,1)} %bitcast.270, f32[2,1,64,8192]{3,2,1,0:T(8,128)} %get-tuple-element.29, f32[2,1,64,8192]{3,2,1,0:T(8,128)} %get-tuple-element.28, f32[8192]{0:T(1024)S(1)} %fusion.101), kind=kOutput, calls=%fused_computation.1 | convolution fusion | flops 2153775104 | bytes 17334272 | tf_op jit(solution)/shard_map/szkp,pftcl->szkftcl/dot_general | solution.py:195
  198.5 0.9 reshape.1156
  199.4 4.8 all-to-all-start
  204.2 2.7 all-to-all-done
  207.1 0.3 copy.127
  207.4 0.4 fusion.30
  207.9 6.6 copy.128
  214.4 13.1 %reshape.1144 = bf16[128,2,2,128,1]{3,0,2,1,4:T(8,128)(2,1)S(1)} reshape(bf16[64,2,2,2,64,2]{5,4,1,0,3,2:T(8,128)(2,1)} %copy.128) | data formatting | bytes 262144 | tf_op jit(solution)/shard_map/convert_element_type | solution.py:89
  228.3 0.3 fusion.43
  228.8 0.5 fusion.44
  229.6 10.0 add.648
  239.6 3.9 copy.141
  243.5 10.0 sub.140
  253.5 3.9 copy.142
  257.4 0.5 fusion.31
  258.1 0.9 reshape.1158
  259.0 5.1 all-to-all-start.1
  264.2 2.3 all-to-all-done.1
  267.2 16.6 %convolution_bitcast_fusion = f32[8192,2,2,2,64]{4,0,3,2,1:T(8,128)} fusion(bf16[2,2,2,2,64,1,64]{6,4,1,0,5,3,2:T(8,128)(2,1)S(1)} %get-tuple-element.27, bf16[2,2,2,2,64,1,64]{6,4,1,0,5,3,2:T(8,128)(2,1)S(1)} %get-tuple-element.26, f32[2,1,64,8192]{3,2,1,0:T(8,128)} %get-tuple-element.29, f32[2,1,64,8192]{3,2,1,0:T(8,128)} %get-tuple-element.28, ...), kind=kOutput, calls=%fused_computation | convolution fusion | flops 2154299392 | bytes 25460736 | tf_op jit(solution)/shard_map/szkp,szftkcl->pftcl/dot_general | solution.py:175
  283.9 1.2 fusion.42
  285.1 721.6 %reduce-scatter.2.cloned.1.call-done = f32[64,2,2,2,64]{4,0,3,2,1:T(8,128)} async-done(((f32[8192,2,2,2,64]{4,0,3,2,1:T(8,128)}), f32[64,2,2,2,64]{4,0,3,2,1:T(8,128)}) %reduce-scatter.2.cloned.1.call-update) | async-done | bytes 131088 | tf_op jit(solution)/shard_map/reduce_scatter | solution.py:214
  1006.7 4.8 fusion.3
  1011.5 2.3 copy.148
  (62 shorter events, 3.5 us)
Async XLA Ops:
  7.2 180.5 %all-gather.2.cloned.1.call-start = ((), (), s32[]{:S(2)}) async-start(), calls=%async_computation.3 | async-start | bytes 16908288 | tf_op jit(solution)/shard_map/all_gather | solution.py:198
  7.8 23.3 %copy-start.4 = (bf16[2,2,64,8192]{3,2,1,0:T(8,128)(2,1)S(1)}, bf16[2,2,64,8192]{3,2,1,0:T(8,128)(2,1)}, u32[]{:S(2)}) copy-start(bf16[2,2,64,8192]{3,2,1,0:T(8,128)(2,1)} %param.5) | copy-start | bytes 12582916
  27.7 2.0 copy-start
  27.8 3.3 copy-start.1
  31.1 3.9 copy-start.3
  31.1 4.1 copy-start.5
  199.4 7.5 all-to-all-start
  214.4 13.9 %copy-start.2 = (bf16[1,4,32,8,256]{4,3,2,1,0:T(8,128)(2,1)S(1)}, bf16[1,4,32,8,256]{4,3,2,1,0:T(8,128)(2,1)}, u32[]{:S(2)}) copy-start(bf16[1,4,32,8,256]{4,3,2,1,0:T(8,128)(2,1)} %param.9) | copy-start | bytes 1572868
  259.0 7.6 all-to-all-start.1
  264.1 742.6 %reduce-scatter.2.cloned.1.call-start = ((), (), s32[]{:S(2)}) async-start(), calls=%async_computation.4 | async-start | bytes 33816576 | tf_op jit(solution)/shard_map/reduce_scatter | solution.py:214
Sparse Core Ops, SparseCore 0:
  34.3 153.3 all-gather.1
  284.0 722.6 reduce-scatter.1
where the time goes:
time: 1020 us
  waiting for transfers between devices  857 us (84%)
  local copies, waits for them, and re-layouts  57 us (6%)
  other arithmetic  45 us (4%)
  matrix products  36.5 us (4%)
  between operations  15.1 us (1%)
    reduce_scatter x1, waiting for transfers between devices, local(): lax.psum_scatter(strip_terms(table_part, paired), ('facet', 'row'), scatt...  722 us
    all_gather x1, waiting for transfers between devices, local(): lax.all_gather(strips, ('facet', 'row'), axis=0, tiled=True)  130 us
    cos x4, other arithmetic, turn_pair(): return (jnp.cos(angle), jnp.sin(angle))  41.6 us
  transfers between devices with their start and end apart: 4, of which 4 were waited for; matrix products, arithmetic and copies ran while one was open for 2% of the time, Pallas kernels for 0%

commit v1 on v0

--- a/solution.py
+++ b/solution.py
@@ -195,7 +195,12 @@
     raw = jnp.einsum(
         "szkp,pftcl->szkftcl",
         table_part,
-        lax.all_gather(strips, ("facet", "row"), axis=0, tiled=True),
+        jnp.concatenate(
+            lax.all_to_all(
+                jnp.stack([strips] * lax.axis_size(("facet", "row"))), ("facet", "row"), 0, 0
+            ),
+            axis=0,
+        ),
         preferred_element_type=jnp.float32,
     )
     contrib = finish_contrib(raw, turn_real, turn_imag)

time: 1020 us -> 1180 us (1.16)
  local copies, waits for them, and re-layouts: 57 us -> 166 us
  waiting for transfers between devices: 857 us -> 886 us
  starting transfers between devices: 9.98 us -> 25.8 us
    all_to_all x0 -> x1, waiting for transfers between devices: none -> 165 us  [local(): lax.all_to_all(jnp.stack([strips] * lax.axis_size(('facet', 'row'))), ('f...]
    all_gather x1 -> x0, waiting for transfers between devices: 130 us -> none  [local(): lax.all_gather(strips, ('facet', 'row'), axis=0, tiled=True)]
    unnamed x18 -> x21, local copies, waits for them, and re-layouts: 7.85 us -> 76.5 us
    reshape x0 -> x1, local copies, waits for them, and re-layouts: none -> 22.5 us  [local(): jnp.concatenate(lax.all_to_all(jnp.stack([strips] * lax.axis_size(('facet...]
    all_to_all x0 -> x1, local copies, waits for them, and re-layouts: none -> 18.6 us  [local(): lax.all_to_all(jnp.stack([strips] * lax.axis_size(('facet', 'row'))), ('f...]
    all_to_all x0 -> x1, starting transfers between devices: none -> 15.6 us  [local(): lax.all_to_all(jnp.stack([strips] * lax.axis_size(('facet', 'row'))), ('f...]
where the time goes in v1:
time: 1180 us; the launch traced here: 1170 us
  waiting for transfers between devices  886 us (75%)
  local copies, waits for them, and re-layouts  166 us (14%)
  other arithmetic  44.8 us (4%)
  matrix products  34.1 us (3%)
  starting transfers between devices  25.8 us (2%)
  between operations  15.5 us (1%)
    reduce_scatter x1, waiting for transfers between devices, local(): lax.psum_scatter(strip_terms(table_part, paired), ('facet', 'row'), scatt...  716 us
    all_to_all x1, waiting for transfers between devices, local(): lax.all_to_all(jnp.stack([strips] * lax.axis_size(('facet', 'row'))), ('f...  165 us
    unnamed x21, local copies, waits for them, and re-layouts  76.5 us
    cos x4, other arithmetic, turn_pair(): return (jnp.cos(angle), jnp.sin(angle))  41.4 us
  transfers between devices with their start and end apart: 4, of which 4 were waited for; matrix products, arithmetic and copies ran while one was open for 2% of the time, Pallas kernels for 0%

profile of v1, /device:TPU:2, one launch (start us, length us, event | category | flops | bytes accessed | tf_op | source)
XLA Modules:
  0.0 1172.2 jit_solution(4635313772098552250)
XLA Ops:
  7.8 19.7 %fusion.29 = (f32[2,1,64,8192]{3,2,1,0:T(8,128)S(1)}, f32[2,1,64,8192]{3,2,1,0:T(8,128)S(1)}) fusion(s32[2,8192]{1,0:T(2,128)S(1)} %get-tuple-element.37, s32[2,8192]{1,0:T(2,128)S(1)} %get-tuple-element.36, s32[64]{0:T(128)S(1)} %iota_multiply_fusion), kind=kLoop, calls=%fused_computation.59 | loop fusion | flops 40894464 | bytes 8519936 | tf_op jit(solution)/shard_map/cos | solution.py:27
  27.5 2.3 fusion.39
  29.8 1.0 copy-done.1
  30.8 16.2 %broadcast_bitcast_fusion = bf16[128,2,2,2,64,64]{5,4,3,2,1,0:T(8,128)(2,1)} fusion(bf16[64,2,2,2,64]{0,4,2,3,1:T(8,128)(2,1)S(1)} %fusion.39), kind=kLoop, calls=%fused_computation.297 | loop fusion | bytes 8454144
  47.1 27.1 %reshape.1163 = bf16[128,2,16384]{2,1,0:T(2,128)(2,1)} reshape(bf16[128,2,2,2,64,64]{5,4,3,2,1,0:T(8,128)(2,1)} %broadcast_bitcast_fusion) | data formatting | bytes 16777216
  74.2 15.6 %all-to-all-start = ((bf16[128,2,16384]{2,1,0:T(2,128)(2,1)}), bf16[128,2,16384]{2,1,0:T(2,128)(2,1)}, u32[]{:S(2)}, u32[]{:S(2)}) async-start(bf16[128,2,16384]{2,1,0:T(2,128)(2,1)} %reshape.1163), calls=%async_computation | async-start | bytes 16777216 | tf_op jit(solution)/shard_map/all_to_all | solution.py:199
  91.5 21.4 %fusion.27 = (f32[2,1,64,8192]{3,2,1,0:T(8,128)}, f32[2,1,64,8192]{3,2,1,0:T(8,128)}) fusion(s32[8192]{0:T(1024)S(1)} %get-tuple-element.44, s32[8192]{0:T(1024)S(1)} %get-tuple-element.45, s32[2,64]{1,0:T(2,128)S(1)} %and_select_fusion.15), kind=kLoop, calls=%fused_computation.57 | loop fusion | flops 40894464 | bytes 8454656 | tf_op jit(solution)/shard_map/cos | solution.py:27
  112.9 165.2 %all-to-all-done = bf16[128,2,16384]{2,1,0:T(2,128)(2,1)} async-done(((bf16[128,2,16384]{2,1,0:T(2,128)(2,1)}), bf16[128,2,16384]{2,1,0:T(2,128)(2,1)}, u32[]{:S(2)}, u32[]{:S(2)}) %all-to-all-start) | async-done | bytes 8388640 | tf_op jit(solution)/shard_map/all_to_all | solution.py:199
  278.1 27.6 %reshape.1164 = bf16[128,2,2,2,64,64]{5,4,3,2,1,0:T(8,128)(2,1)} reshape(bf16[128,2,16384]{2,1,0:T(2,128)(2,1)} %all-to-all-done) | data formatting | bytes 16777216
  305.7 18.6 %copy.127 = bf16[128,64,2,2,2,64]{1,0,5,4,3,2:T(8,128)(2,1)} copy(bf16[128,64,2,2,2,64]{1,5,4,3,2,0:T(8,128)(2,1)} %bitcast.276) | data formatting | bytes 16777216 | tf_op jit(solution)/shard_map/all_to_all | solution.py:199
  324.3 22.5 %reshape.1146 = bf16[8192,2,2,2,64,1,1]{0,4,3,2,1,5,6:T(8,128)(2,1)} reshape(bf16[128,64,2,2,2,64]{1,0,5,4,3,2:T(8,128)(2,1)} %copy.127) | data formatting | bytes 16777216 | tf_op jit(solution)/shard_map/reshape | solution.py:198
  346.9 8.2 fusion.4
  355.4 0.9 reshape.1165
  356.3 4.8 all-to-all-start.1
  361.1 2.5 all-to-all-done.1
  364.1 0.4 fusion.31
  364.5 6.6 copy.132
  371.0 13.1 %reshape.1150 = bf16[128,2,2,128,1]{3,0,2,1,4:T(8,128)(2,1)S(1)} reshape(bf16[64,2,2,2,64,2]{5,4,1,0,3,2:T(8,128)(2,1)} %copy.132) | data formatting | bytes 262144 | tf_op jit(solution)/shard_map/convert_element_type | solution.py:89
  385.4 0.5 fusion.49
  386.2 10.0 sub.140
  396.2 3.9 copy.146
  400.1 10.0 add.648
  410.1 3.9 copy.145
  414.0 0.5 fusion.32
  414.7 0.9 reshape.1167
  415.6 5.4 all-to-all-start.2
  421.1 2.3 all-to-all-done.2
  424.1 16.6 %convolution_bitcast_fusion = f32[8192,2,2,2,64]{4,0,3,2,1:T(8,128)} fusion(bf16[2,2,2,2,64,1,64]{6,4,1,0,5,3,2:T(8,128)(2,1)S(1)} %get-tuple-element.27, bf16[2,2,2,2,64,1,64]{6,4,1,0,5,3,2:T(8,128)(2,1)S(1)} %get-tuple-element.26, f32[2,1,64,8192]{3,2,1,0:T(8,128)} %get-tuple-element.29, f32[2,1,64,8192]{3,2,1,0:T(8,128)} %get-tuple-element.28, ...), kind=kOutput, calls=%fused_computation | convolution fusion | flops 2154299392 | bytes 25460736 | tf_op jit(solution)/shard_map/szkp,szftkcl->pftcl/dot_general | solution.py:175
  440.8 1.2 fusion.47
  441.9 716.0 %reduce-scatter.2.cloned.1.call-done = f32[64,2,2,2,64]{4,0,3,2,1:T(8,128)} async-done(((f32[8192,2,2,2,64]{4,0,3,2,1:T(8,128)}), f32[64,2,2,2,64]{4,0,3,2,1:T(8,128)}) %reduce-scatter.2.cloned.1.call-update) | async-done | bytes 131088 | tf_op jit(solution)/shard_map/reduce_scatter | solution.py:219
  1157.9 4.8 fusion.1
  1162.7 2.3 copy.152
  (65 shorter events, 4.8 us)
Async XLA Ops:
  7.8 19.8 %copy-start.4 = (bf16[2,2,64,8192]{3,2,1,0:T(8,128)(2,1)S(1)}, bf16[2,2,64,8192]{3,2,1,0:T(8,128)(2,1)}, u32[]{:S(2)}) copy-start(bf16[2,2,64,8192]{3,2,1,0:T(8,128)(2,1)} %param.5) | copy-start | bytes 12582916
  27.5 2.3 copy-start
  27.5 3.3 copy-start.1
  74.2 16.2 %copy-start.3 = (s32[1,4]{1,0:T(1,128)S(1)}, s32[1,4]{1,0:T(1,128)}, u32[]{:S(2)}) copy-start(s32[1,4]{1,0:T(1,128)} %param.7) | copy-start | bytes 52
  74.2 16.6 %copy-start.5 = (s32[256]{0:T(256)S(1)}, s32[256]{0:T(256)}, u32[]{:S(2)}) copy-start(s32[256]{0:T(256)} %param.6) | copy-start | bytes 3076
  74.2 203.9 %all-to-all-start = ((bf16[128,2,16384]{2,1,0:T(2,128)(2,1)}), bf16[128,2,16384]{2,1,0:T(2,128)(2,1)}, u32[]{:S(2)}, u32[]{:S(2)}) async-start(bf16[128,2,16384]{2,1,0:T(2,128)(2,1)} %reshape.1163), calls=%async_computation | async-start | bytes 16777216 | tf_op jit(solution)/shard_map/all_to_all | solution.py:199
  356.3 7.3 all-to-all-start.1
  371.0 13.9 %copy-start.2 = (bf16[1,4,32,8,256]{4,3,2,1,0:T(8,128)(2,1)S(1)}, bf16[1,4,32,8,256]{4,3,2,1,0:T(8,128)(2,1)}, u32[]{:S(2)}) copy-start(bf16[1,4,32,8,256]{4,3,2,1,0:T(8,128)(2,1)} %param.9) | copy-start | bytes 1572868
  415.6 7.8 all-to-all-start.2
  421.0 736.9 %reduce-scatter.2.cloned.1.call-start = ((), (), s32[]{:S(2)}) async-start(), calls=%async_computation.4 | async-start | bytes 33816576 | tf_op jit(solution)/shard_map/reduce_scatter | solution.py:219
Sparse Core Ops, SparseCore 0:
  440.9 716.9 reduce-scatter.1
